TPU v7x, 512 devices: a whole 4x4x16 slice. The times are simulated.
512 devices in a mesh: lev: 16 (over x, z_hi, core), hor: 32 (over z_lo, y).
Axes of the slice: x: 4, y: 4, z: 16 (z_hi: 2, z_lo: 8; z = z_hi * 8 + z_lo), core: 2. Of those that a mesh axis runs over, the one named last changes fastest.
Arguments:
- state: float32 [2, 128, 512, 1024], P(None, 'lev', 'hor'), may hold values from -6 to 6
- cotangent: bfloat16 [2, 128, 512, 1024], P(None, 'lev', 'hor'), may hold values from -6 to 6
- diffusion: float32 [128, 512, 1024], P('lev', 'hor'), may hold values from 0.02 to 0.2
- vertical_inverse: float32 [2, 128, 128], replicated, may hold values from -0.2 to 2
- w_in: bfloat16 [1024, 256], replicated, may hold values from -0.375 to 0.375
- w_out: bfloat16 [256, 1024], replicated, may hold values from -0.1875 to 0.1875
Outputs:
- state_adjoint: float32 [2, 128, 512, 1024], P(None, 'lev', 'hor')
All inputs are finite; a program needn't handle non-finite values.
Results may differ from a plain program's by a relative error of at most 0.002.
Values may be sent and summed in bfloat16 or wider, within the bound.
A program may use at most 64 MiB of HBM per device.

v0:
```python
import jax
import jax.numpy as jnp
from jax import lax
from jax.sharding import PartitionSpec as P


def with_halo(block, sides, width):
    for axis, dim in sides:
        count = lax.axis_size(axis)
        forward = [(i, i + 1) for i in range(count - 1)]
        backward = [(target, source) for source, target in forward]
        low = lax.ppermute(
            lax.slice_in_dim(block, block.shape[dim] - width, None, axis=dim), axis, forward
        )
        high = lax.ppermute(lax.slice_in_dim(block, 0, width, axis=dim), axis, backward)
        block = jnp.concatenate([low, block, high], axis=dim)
    return block


def laplace_local(extended):
    padded = jnp.pad(extended, ((0, 0), (0, 0), (0, 0), (1, 1)))
    return (
        padded[:, :, 2:, 1:-1]
        + padded[:, :, :-2, 1:-1]
        + padded[:, :, 1:-1, 2:]
        + padded[:, :, 1:-1, :-2]
        - 4.0 * padded[:, :, 1:-1, 1:-1]
    )


def column_adjoint(diffused, cot_block, vertical_inverse, w_in, w_out):
    highest = lax.Precision.HIGHEST
    solved = jnp.einsum("fkl,flc->fkc", vertical_inverse, diffused, precision=highest)
    fields, levels, count = solved.shape
    inputs = solved.reshape(fields * levels, count).astype(jnp.bfloat16)
    preact = jnp.dot(w_in, inputs, preferred_element_type=jnp.float32)
    cot_cols = cot_block.reshape(fields * levels, count)
    hidden_grad = lax.dot_general(
        w_out, cot_cols, (((0,), (0,)), ((), ())), preferred_element_type=jnp.float32
    )
    squashed = jax.nn.sigmoid(preact)
    pre_grad = (hidden_grad * squashed * (1.0 + preact * (1.0 - squashed))).astype(jnp.bfloat16)
    level_grad = cot_cols.astype(jnp.float32) + lax.dot_general(
        w_in, pre_grad, (((0,), (0,)), ((), ())), preferred_element_type=jnp.float32
    )
    level_grad = level_grad.reshape(fields, levels, count)
    return jnp.einsum("fkl,fkc->flc", vertical_inverse, level_grad, precision=highest)


def body(state, cotangent, diffusion, vertical_inverse, w_in, w_out):
    extended = with_halo(state, (("hor", 2),), 1)
    diffused = state + diffusion[None] * laplace_local(extended)
    state_cols = lax.all_to_all(diffused, "lev", split_axis=3, concat_axis=1, tiled=True)
    cot_cols = lax.all_to_all(cotangent, "lev", split_axis=3, concat_axis=1, tiled=True)
    shape_cols = state_cols.shape
    flat_state = state_cols.reshape(shape_cols[0], shape_cols[1], shape_cols[2] * shape_cols[3])
    flat_cot = cot_cols.reshape(shape_cols[0], shape_cols[1], shape_cols[2] * shape_cols[3])
    adjoint_cols = column_adjoint(flat_state, flat_cot, vertical_inverse, w_in, w_out).reshape(
        shape_cols
    )
    adjoint_levels = lax.all_to_all(adjoint_cols, "lev", split_axis=1, concat_axis=3, tiled=True)
    weighted = diffusion[None] * adjoint_levels
    rimmed = with_halo(weighted, (("hor", 2),), 1)
    return adjoint_levels + laplace_local(rimmed)


def solution(mesh):
    placed = (
        P(None, "lev", "hor", None),
        P(None, "lev", "hor", None),
        P("lev", "hor", None),
        P(),
        P(),
        P(),
    )
    return jax.shard_map(
        body, mesh=mesh, in_specs=placed, out_specs=P(None, "lev", "hor", None), check_vma=False
    )
```

profile of v0, /device:TPU:32, one launch (start us, length us, event | category | flops | bytes accessed | tf_op | source)
XLA Modules:
  0.0 259.4 jit_solution(9660499994656659942)
XLA Ops:
  0.0 5.8 %copy.21 = bf16[2,8,16,1024]{2,1,0,3:T(8,128)(2,1)} copy(bf16[2,8,16,1024]{3,2,1,0:T(8,128)(2,1)} %param.7) | data formatting | bytes 1048576 | tf_op args[1]
  5.8 6.5 %reshape.19 = bf16[16,2,8192]{2,1,0:T(2,128)(2,1)} reshape(bf16[1024,2,8,16]{3,2,1,0:T(8,128)(2,1)} %bitcast.61) | data formatting | bytes 1048576
  12.3 16.8 %all-to-all-start = ((bf16[16,2,8192]{2,1,0:T(2,128)(2,1)}), bf16[16,2,8192]{2,1,0:T(2,128)(2,1)}, u32[]{:S(2)}, u32[]{:S(2)}) async-start(bf16[16,2,8192]{2,1,0:T(2,128)(2,1)} %reshape.19), calls=%async_computation | async-start | bytes 1048576 | tf_op jit(solution)/shard_map/all_to_all | solution.py:54
  29.1 0.0 copy-start.2
  29.1 0.1 fusion.17
  29.2 5.5 %collective-permute-start = (f32[2,8,1,1024]{3,2,1,0:T(1,128)S(1)}, f32[2,8,1,1024]{3,2,1,0:T(1,128)S(1)}, u32[]{:S(2)}, u32[]{:S(2)}) collective-permute-start(f32[2,8,1,1024]{3,2,1,0:T(1,128)S(1)} %get-tuple-element.8), channel_id=1, source_target_pairs={{1,0},{2,1},{3,2},{4,3},{5,4},{6,5},{7,6},{8,7},{9,8},{10,9},{11,1... | collective-permute-start | bytes 196616 | tf_op jit(solution)/shard_map/ppermute | solution.py:15
  34.7 1.9 collective-permute-start.1
  36.7 17.3 %collective-permute-done = f32[2,8,1,1024]{3,2,1,0:T(1,128)S(1)} collective-permute-done((f32[2,8,1,1024]{3,2,1,0:T(1,128)S(1)}, f32[2,8,1,1024]{3,2,1,0:T(1,128)S(1)}, u32[]{:S(2)}, u32[]{:S(2)}) %collective-permute-start) | collective-permute-done | bytes 65568 | tf_op jit(solution)/shard_map/ppermute | solution.py:15
  53.9 0.0 collective-permute-done.1
  53.9 0.9 select_maximum_fusion.2
  54.9 0.7 fusion.13
  55.6 6.1 %copy.23 = f32[2,8,16,1024]{2,1,0,3:T(8,128)} copy(f32[2,8,16,1024]{3,2,1,0:T(8,128)S(1)} %fusion.13) | data formatting | bytes 2097152 | tf_op jit(solution)/shard_map/add | solution.py:52
  61.7 7.1 %reshape.17 = f32[16,1,16384]{2,1,0:T(1,128)} reshape(f32[1024,2,8,16]{3,2,1,0:T(8,128)} %bitcast.59) | data formatting | bytes 2097152
  68.9 0.0 all-to-all-done
  68.9 14.2 %all-to-all-start.1 = ((f32[16,1,16384]{2,1,0:T(1,128)}), f32[16,1,16384]{2,1,0:T(1,128)S(1)}, u32[]{:S(2)}, u32[]{:S(2)}) async-start(f32[16,1,16384]{2,1,0:T(1,128)} %reshape.17), calls=%async_computation.1 | async-start | bytes 2097152 | tf_op jit(solution)/shard_map/all_to_all | solution.py:53
  83.0 5.4 %reshape.20 = bf16[1024,2,8,16]{3,2,1,0:T(8,128)(2,1)} reshape(bf16[16,2,8192]{2,1,0:T(2,128)(2,1)} %all-to-all-done) | data formatting | bytes 1048576
  88.4 4.0 %copy.22 = bf16[2,8,16,16,64]{4,2,1,3,0:T(8,128)(2,1)S(1)} copy(bf16[2,8,16,16,64]{2,1,0,4,3:T(8,128)(2,1)} %bitcast.60) | data formatting | bytes 1048576 | tf_op jit(solution)/shard_map/all_to_all | solution.py:54
  92.4 1.6 reshape_reshape.3
  94.0 45.7 %all-to-all-done.1 = f32[16,1,16384]{2,1,0:T(1,128)S(1)} async-done(((f32[16,1,16384]{2,1,0:T(1,128)}), f32[16,1,16384]{2,1,0:T(1,128)S(1)}, u32[]{:S(2)}, u32[]{:S(2)}) %all-to-all-start.1) | async-done | bytes 1048608 | tf_op jit(solution)/shard_map/all_to_all | solution.py:53
  139.7 0.6 broadcast.42
  140.3 3.1 %reduce = f32[16,16384]{1,0:T(8,128)S(1)} reduce(f32[16,1,16384]{2,1,0:T(1,128)S(1)} %all-to-all-done.1, f32[]{:T(128)} %broadcast.42), dimensions={1}, to_apply=%all_to_all.38.reduce_sub_computation | reduce | bytes 2097156 | tf_op jit(solution)/shard_map/all_to_all | solution.py:53
  143.4 4.8 %reshape.18 = f32[1024,2,8,16]{3,2,1,0:T(8,128)} reshape(f32[16,16384]{1,0:T(8,128)S(1)} %reduce) | data formatting | bytes 2097152
  148.2 5.4 %copy.24 = f32[2,8,16,16,64]{4,2,1,3,0:T(8,128)S(1)} copy(f32[2,8,16,16,64]{2,1,0,4,3:T(8,128)} %bitcast.58) | data formatting | bytes 2097152 | tf_op jit(solution)/shard_map/all_to_all | solution.py:53
  153.6 0.0 copy-start.4
  153.6 1.5 reshape.14
  155.2 2.3 convolution_convert_fusion
  157.4 0.0 copy-done
  157.4 0.0 copy-start.3
  157.5 0.0 copy-start.5
  157.5 2.7 %fusion.19 = f32[1024,1024]{0,1:T(8,128)} fusion(bf16[1024,256]{1,0:T(8,128)(2,1)S(1)} %copy-done, bf16[256,1024]{1,0:T(8,128)(2,1)S(1)} %bitcast.67), kind=kOutput, calls=%fused_computation.38 | convolution fusion | flops 536870912 | bytes 5242880 | tf_op jit(solution)/shard_map/dot_general | solution.py:36
  160.1 0.0 copy-done.5
  160.1 4.4 %fusion.7 = f32[256,1024]{1,0:T(8,128)S(1)} fusion(bf16[1024,256]{1,0:T(8,128)(2,1)S(1)} %copy-done, f32[1024,1024]{0,1:T(8,128)} %fusion.19, bf16[256,1024]{1,0:T(8,128)(2,1)S(1)} %copy-done.5, bf16[256,1024]{1,0:T(8,128)(2,1)S(1)} %copy-done.3), kind=kOutput, calls=%fused_computation.16 | convolution fusion | flops 1083703296 | bytes 6815744 | tf_op jit(solution)/shard_map/dot_general | solution.py:43
  164.6 2.8 %fusion.18 = f32[2,1024,128]{2,1,0:T(8,128)} fusion(f32[2,128,1024]{2,1,0:T(8,128)S(1)} %bitcast.68, f32[2,128,128]{2,1,0:T(8,128)S(1)} %copy-done.4), kind=kOutput, calls=%fused_computation.37 | convolution fusion | flops 402653184 | bytes 2228224 | tf_op jit(solution)/shard_map/fkl,fkc->flc/dot_general | solution.py:47
  167.3 3.1 %copy.27 = f32[2,128,16,64]{3,2,0,1:T(8,128)S(1)} copy(f32[2,128,16,64]{1,3,2,0:T(8,128)} %bitcast.66) | data formatting | bytes 2097152 | tf_op jit(solution)/shard_map/reshape | solution.py:58
  170.4 2.3 reshape.21
  172.7 62.7 %all_to_all.48 = f32[16,1,16384]{2,1,0:T(1,128)S(1)} all-to-all(f32[16,1,16384]{2,1,0:T(1,128)} %reshape.21), channel_id=1, replica_groups=mesh['lev'=16,'hor'=32] {'lev'}, dimensions={0} | all-to-all | bytes 2097152 | tf_op jit(solution)/shard_map/all_to_all | solution.py:61
  235.4 4.4 %reduce.1 = f32[16,16384]{1,0:T(8,128)} reduce(f32[16,1,16384]{2,1,0:T(1,128)S(1)} %all_to_all.48, f32[]{:T(128)} %broadcast.42), dimensions={1}, to_apply=%all_to_all.41.reduce_sub_computation | reduce | bytes 2097156 | tf_op jit(solution)/shard_map/all_to_all | solution.py:61
  239.7 2.1 reshape.22
  241.8 2.6 copy.29
  244.3 2.0 all_to_all.44
  246.4 0.1 broadcast_multiply_fusion
  246.5 0.1 fusion.16
  246.6 1.9 collective-permute-start.2
  248.5 3.9 %collective-permute-start.3 = (f32[2,8,1,1024]{3,2,1,0:T(1,128)S(1)}, f32[2,8,1,1024]{3,2,1,0:T(1,128)S(1)}, u32[]{:S(2)}, u32[]{:S(2)}) collective-permute-start(f32[2,8,1,1024]{3,2,1,0:T(1,128)S(1)} %get-tuple-element.5), channel_id=1, source_target_pairs={{0,1},{1,2},{2,3},{3,4},{4,5},{5,6},{6,7},{7,8},{8,9},{9,10},{10,1... | collective-permute-start | bytes 196616 | tf_op jit(solution)/shard_map/ppermute | solution.py:12
  252.4 0.3 collective-permute-done.2
  252.7 4.0 %collective-permute-done.3 = f32[2,8,1,1024]{3,2,1,0:T(1,128)S(1)} collective-permute-done((f32[2,8,1,1024]{3,2,1,0:T(1,128)S(1)}, f32[2,8,1,1024]{3,2,1,0:T(1,128)S(1)}, u32[]{:S(2)}, u32[]{:S(2)}) %collective-permute-start.3) | collective-permute-done | bytes 65568 | tf_op jit(solution)/shard_map/ppermute | solution.py:12
  256.8 0.9 select_maximum_fusion
  257.7 1.7 fusion.9
  (6 shorter events, 0.0 us)
Async XLA Ops:
  0.0 157.4 %copy-start = (bf16[1024,256]{1,0:T(8,128)(2,1)S(1)}, bf16[1024,256]{1,0:T(8,128)(2,1)}, u32[]{:S(2)}) copy-start(bf16[1024,256]{1,0:T(8,128)(2,1)} %param.10) | copy-start | bytes 1572868
  5.8 23.3 %copy-start.1 = (f32[2,8,16,1024]{3,2,1,0:T(8,128)S(1)}, f32[2,8,16,1024]{3,2,1,0:T(8,128)}, u32[]{:S(2)}) copy-start(f32[2,8,16,1024]{3,2,1,0:T(8,128)} %param.6) | copy-start | bytes 3145732
  12.3 56.6 %all-to-all-start = ((bf16[16,2,8192]{2,1,0:T(2,128)(2,1)}), bf16[16,2,8192]{2,1,0:T(2,128)(2,1)}, u32[]{:S(2)}, u32[]{:S(2)}) async-start(bf16[16,2,8192]{2,1,0:T(2,128)(2,1)} %reshape.19), calls=%async_computation | async-start | bytes 1048576 | tf_op jit(solution)/shard_map/all_to_all | solution.py:54
  29.1 25.7 %copy-start.2 = (f32[8,16,1024]{2,1,0:T(8,128)S(1)}, f32[8,16,1024]{2,1,0:T(8,128)}, u32[]{:S(2)}) copy-start(f32[8,16,1024]{2,1,0:T(8,128)} %param.8) | copy-start | bytes 1572868
  29.2 24.7 %collective-permute-start = (f32[2,8,1,1024]{3,2,1,0:T(1,128)S(1)}, f32[2,8,1,1024]{3,2,1,0:T(1,128)S(1)}, u32[]{:S(2)}, u32[]{:S(2)}) collective-permute-start(f32[2,8,1,1024]{3,2,1,0:T(1,128)S(1)} %get-tuple-element.8), channel_id=1, source_target_pairs={{1,0},{2,1},{3,2},{4,3},{5,4},{6,5},{7,6},{8,7},{9,8},{10,9},{11,1... | collective-permute-start | bytes 196616 | tf_op jit(solution)/shard_map/ppermute | solution.py:15
  34.7 19.2 %collective-permute-start.1 = (f32[2,8,1,1024]{3,2,1,0:T(1,128)S(1)}, f32[2,8,1,1024]{3,2,1,0:T(1,128)S(1)}, u32[]{:S(2)}, u32[]{:S(2)}) collective-permute-start(f32[2,8,1,1024]{3,2,1,0:T(1,128)S(1)} %get-tuple-element.7), channel_id=1, source_target_pairs={{0,1},{1,2},{2,3},{3,4},{4,5},{5,6},{6,7},{7,8},{8,9},{9,10},{10,1... | collective-permute-start | bytes 196616 | tf_op jit(solution)/shard_map/ppermute | solution.py:12
  68.9 70.9 %all-to-all-start.1 = ((f32[16,1,16384]{2,1,0:T(1,128)}), f32[16,1,16384]{2,1,0:T(1,128)S(1)}, u32[]{:S(2)}, u32[]{:S(2)}) async-start(f32[16,1,16384]{2,1,0:T(1,128)} %reshape.17), calls=%async_computation.1 | async-start | bytes 2097152 | tf_op jit(solution)/shard_map/all_to_all | solution.py:53
  153.6 1.6 copy-start.4
  157.4 2.7 %copy-start.3 = (bf16[256,1024]{1,0:T(8,128)(2,1)S(1)}, bf16[256,1024]{1,0:T(8,128)(2,1)}, u32[]{:S(2)}) copy-start(bf16[256,1024]{1,0:T(8,128)(2,1)} %reshape_reshape.3) | copy-start | bytes 1572868
  157.5 2.7 %copy-start.5 = (bf16[256,1024]{1,0:T(8,128)(2,1)S(1)}, bf16[256,1024]{1,0:T(8,128)(2,1)}, u32[]{:S(2)}) copy-start(bf16[256,1024]{1,0:T(8,128)(2,1)} %param.11) | copy-start | bytes 1572868
  246.6 6.2 %collective-permute-start.2 = (f32[2,8,1,1024]{3,2,1,0:T(1,128)S(1)}, f32[2,8,1,1024]{3,2,1,0:T(1,128)S(1)}, u32[]{:S(2)}, u32[]{:S(2)}) collective-permute-start(f32[2,8,1,1024]{3,2,1,0:T(1,128)S(1)} %get-tuple-element.6), channel_id=1, source_target_pairs={{1,0},{2,1},{3,2},{4,3},{5,4},{6,5},{7,6},{8,7},{9,8},{10,9},{11,1... | collective-permute-start | bytes 196616 | tf_op jit(solution)/shard_map/ppermute | solution.py:15
  248.5 8.3 %collective-permute-start.3 = (f32[2,8,1,1024]{3,2,1,0:T(1,128)S(1)}, f32[2,8,1,1024]{3,2,1,0:T(1,128)S(1)}, u32[]{:S(2)}, u32[]{:S(2)}) collective-permute-start(f32[2,8,1,1024]{3,2,1,0:T(1,128)S(1)} %get-tuple-element.5), channel_id=1, source_target_pairs={{0,1},{1,2},{2,3},{3,4},{4,5},{5,6},{6,7},{7,8},{8,9},{9,10},{10,1... | collective-permute-start | bytes 196616 | tf_op jit(solution)/shard_map/ppermute | solution.py:12
where the time goes:
time: 260 us; the launch traced here: 259 us
  waiting for transfers between devices  67.3 us (26%)
  blocking collectives  62.7 us (24%)
  local copies, waits for them, and re-layouts  60.9 us (23%)
  starting transfers between devices  44.2 us (17%)
  matrix products  12.1 us (5%)
  other arithmetic  11.8 us (5%)
    all_to_all x1, blocking collectives, body(): lax.all_to_all(adjoint_cols, 'lev', split_axis=1, concat_axis=3, tiled=True)  62.7 us
    all_to_all x1, waiting for transfers between devices, body(): lax.all_to_all(diffused, 'lev', split_axis=3, concat_axis=1, tiled=True)  45.7 us
    unnamed x19, local copies, waits for them, and re-layouts  33.9 us
    ppermute x2, waiting for transfers between devices, with_halo(): lax.ppermute(lax.slice_in_dim(block, 0, width, axis=dim), axis, backward)  17.6 us
    all_to_all x1, starting transfers between devices, body(): lax.all_to_all(cotangent, 'lev', split_axis=3, concat_axis=1, tiled=True)  16.8 us
    all_to_all x1, starting transfers between devices, body(): lax.all_to_all(diffused, 'lev', split_axis=3, concat_axis=1, tiled=True)  14.2 us
    ppermute x2, starting transfers between devices, with_halo(): lax.ppermute(lax.slice_in_dim(block, 0, width, axis=dim), axis, backward)  7.42 us
    add x1, local copies, waits for them, and re-layouts, body(): diffused = state + diffusion[None] * laplace_local(extended)  6.14 us
  transfers between devices with their start and end apart: 6, of which 4 were waited for; matrix products, arithmetic and copies ran while one was open for 10% of the time, Pallas kernels for 0%

commit v1 on v0

--- a/solution.py
+++ b/solution.py
@@ -50,7 +50,10 @@
 def body(state, cotangent, diffusion, vertical_inverse, w_in, w_out):
     extended = with_halo(state, (("hor", 2),), 1)
     diffused = state + diffusion[None] * laplace_local(extended)
-    state_cols = lax.all_to_all(diffused, "lev", split_axis=3, concat_axis=1, tiled=True)
+    size = lax.axis_size("lev")
+    pieces = jnp.stack(jnp.split(diffused, size, axis=3), axis=0)
+    pieces = lax.all_to_all(pieces, "lev", split_axis=0, concat_axis=0)
+    state_cols = jnp.concatenate(pieces, axis=1)
     cot_cols = lax.all_to_all(cotangent, "lev", split_axis=3, concat_axis=1, tiled=True)
     shape_cols = state_cols.shape
     flat_state = state_cols.reshape(shape_cols[0], shape_cols[1], shape_cols[2] * shape_cols[3])

time: 260 us -> 212 us (0.82)
  the two profiles are of different devices: /device:TPU:32 before, /device:TPU:24 now
where the time goes in v1:
time: 212 us; the launch traced here: 211 us
  starting transfers between devices  73.3 us (35%)
  local copies, waits for them, and re-layouts  46 us (22%)
  waiting for transfers between devices  35.7 us (17%)
  blocking collectives  32 us (15%)
  other arithmetic  12.9 us (6%)
  matrix products  11.1 us (5%)
    ppermute x2, starting transfers between devices, with_halo(): lax.ppermute(lax.slice_in_dim(block, block.shape[dim] - width, None, axis...  47.3 us
    all_to_all x1, blocking collectives, body(): lax.all_to_all(adjoint_cols, 'lev', split_axis=1, concat_axis=3, tiled=True)  32 us
    unnamed x32, local copies, waits for them, and re-layouts  27 us
    all_to_all x1, starting transfers between devices, body(): lax.all_to_all(cotangent, 'lev', split_axis=3, concat_axis=1, tiled=True)  17.8 us
    all_to_all x1, waiting for transfers between devices, body(): lax.all_to_all(cotangent, 'lev', split_axis=3, concat_axis=1, tiled=True)  15.1 us
    all_to_all x1, waiting for transfers between devices, body(): pieces = lax.all_to_all(pieces, 'lev', split_axis=0, concat_axis=0)  14.2 us
    ppermute x2, waiting for transfers between devices, with_halo(): lax.ppermute(lax.slice_in_dim(block, 0, width, axis=dim), axis, backward)  6.33 us
    dot_general x1, matrix products, column_adjoint(): lax.dot_general(w_in, pre_grad, (((0,), (0,)), ((), ())), preferred_eleme...  4.6 us
  transfers between devices with their start and end apart: 6, of which 3 were waited for; matrix products, arithmetic and copies ran while one was open for 13% of the time, Pallas kernels for 0%

profile of v1, /device:TPU:24, one launch (start us, length us, event | category | flops | bytes accessed | tf_op | source)
XLA Modules:
  0.0 211.3 jit_solution(12131683830835069768)
XLA Ops:
  0.0 1.4 fusion.33
  1.4 3.5 %collective-permute-start.1 = (f32[2,8,1,1024]{3,2,1,0:T(1,128)S(1)}, f32[2,8,1,1024]{3,2,1,0:T(1,128)S(1)}, u32[]{:S(2)}, u32[]{:S(2)}) collective-permute-start(f32[2,8,1,1024]{3,2,1,0:T(1,128)S(1)} %get-tuple-element.7), channel_id=1, source_target_pairs={{0,1},{1,2},{2,3},{3,4},{4,5},{5,6},{6,7},{7,8},{8,9},{9,10},{10,1... | collective-permute-start | bytes 196616 | tf_op jit(solution)/shard_map/ppermute | solution.py:12
  4.9 2.4 %collective-permute-start = (f32[2,8,1,1024]{3,2,1,0:T(1,128)S(1)}, f32[2,8,1,1024]{3,2,1,0:T(1,128)S(1)}, u32[]{:S(2)}, u32[]{:S(2)}) collective-permute-start(f32[2,8,1,1024]{3,2,1,0:T(1,128)S(1)} %get-tuple-element.8), channel_id=1, source_target_pairs={{1,0},{2,1},{3,2},{4,3},{5,4},{6,5},{7,6},{8,7},{9,8},{10,9},{11,1... | collective-permute-start | bytes 196616 | tf_op jit(solution)/shard_map/ppermute | solution.py:15
  7.2 5.7 %copy.21 = bf16[2,8,16,1024]{2,1,0,3:T(8,128)(2,1)} copy(bf16[2,8,16,1024]{3,2,1,0:T(8,128)(2,1)} %param.7) | data formatting | bytes 1048576 | tf_op args[1]
  12.9 6.5 %reshape.18 = bf16[16,2,8192]{2,1,0:T(2,128)(2,1)} reshape(bf16[1024,2,8,16]{3,2,1,0:T(8,128)(2,1)} %bitcast.120) | data formatting | bytes 1048576
  19.4 17.8 %all-to-all-start = ((bf16[16,2,8192]{2,1,0:T(2,128)(2,1)}), bf16[16,2,8192]{2,1,0:T(2,128)(2,1)}, u32[]{:S(2)}, u32[]{:S(2)}) async-start(bf16[16,2,8192]{2,1,0:T(2,128)(2,1)} %reshape.18), calls=%async_computation | async-start | bytes 1048576 | tf_op jit(solution)/shard_map/all_to_all | solution.py:57
  37.3 0.0 collective-permute-done.1
  37.3 0.9 select_maximum_fusion.2
  38.2 0.7 fusion.13
  39.0 0.1 fusion.29
  39.1 0.1 fusion.27
  39.2 0.1 fusion.25
  39.4 0.1 fusion.23
  39.5 0.1 fusion.21
  39.6 0.1 fusion.19
  39.7 0.1 fusion.17
  39.9 0.1 fusion.15
  40.0 2.3 %reshape.16 = f32[16,1,16384]{2,1,0:T(1,128)} reshape(f32[16,2,8,16,64]{4,3,2,1,0:T(8,128)S(1)} %fusion.15) | data formatting | bytes 2097152
  42.2 15.1 %all-to-all-done = bf16[16,2,8192]{2,1,0:T(2,128)(2,1)} async-done(((bf16[16,2,8192]{2,1,0:T(2,128)(2,1)}), bf16[16,2,8192]{2,1,0:T(2,128)(2,1)}, u32[]{:S(2)}, u32[]{:S(2)}) %all-to-all-start) | async-done | bytes 524320 | tf_op jit(solution)/shard_map/all_to_all | solution.py:57
  57.4 3.8 %all-to-all-start.1 = ((f32[16,1,16384]{2,1,0:T(1,128)}), f32[16,1,16384]{2,1,0:T(1,128)S(1)}, u32[]{:S(2)}, u32[]{:S(2)}) async-start(f32[16,1,16384]{2,1,0:T(1,128)} %reshape.16), calls=%async_computation.1 | async-start | bytes 2097152 | tf_op jit(solution)/shard_map/all_to_all | solution.py:55
  61.2 5.4 %reshape.19 = bf16[1024,2,8,16]{3,2,1,0:T(8,128)(2,1)} reshape(bf16[16,2,8192]{2,1,0:T(2,128)(2,1)} %all-to-all-done) | data formatting | bytes 1048576
  66.6 4.0 %copy.22 = bf16[2,8,16,16,64]{4,2,1,3,0:T(8,128)(2,1)S(1)} copy(bf16[2,8,16,16,64]{2,1,0,4,3:T(8,128)(2,1)} %bitcast.119) | data formatting | bytes 1048576 | tf_op jit(solution)/shard_map/all_to_all | solution.py:57
  70.6 1.5 reshape_reshape.6
  72.1 14.2 %all-to-all-done.1 = f32[16,1,16384]{2,1,0:T(1,128)S(1)} async-done(((f32[16,1,16384]{2,1,0:T(1,128)}), f32[16,1,16384]{2,1,0:T(1,128)S(1)}, u32[]{:S(2)}, u32[]{:S(2)}) %all-to-all-start.1) | async-done | bytes 1048608 | tf_op jit(solution)/shard_map/all_to_all | solution.py:55
  86.3 0.5 broadcast.42
  86.8 4.3 %reduce = f32[16,16384]{1,0:T(8,128)} reduce(f32[16,1,16384]{2,1,0:T(1,128)S(1)} %all-to-all-done.1, f32[]{:T(128)} %broadcast.42), dimensions={1}, to_apply=%all_to_all.30.reduce_sub_computation | reduce | bytes 2097156 | tf_op jit(solution)/shard_map/all_to_all | solution.py:55
  91.1 2.1 reshape.17
  93.2 1.5 copy.23
  94.7 2.3 %reshape_reshape.7 = f32[2,128,1024]{2,1,0:T(8,128)S(1)} reshape(f32[2,16,8,16,64]{4,3,2,1,0:T(8,128)} %copy.23) | data formatting | bytes 2097152 | tf_op jit(solution)/shard_map/reshape;reshape | solution.py:59
  97.0 1.1 convolution_convert_fusion
  98.1 2.7 %fusion.35 = f32[1024,1024]{0,1:T(8,128)} fusion(bf16[1024,256]{1,0:T(8,128)(2,1)S(1)} %copy-done, bf16[256,1024]{1,0:T(8,128)(2,1)S(1)} %bitcast.126), kind=kOutput, calls=%fused_computation.70 | convolution fusion | flops 536870912 | bytes 5242880 | tf_op jit(solution)/shard_map/dot_general | solution.py:36
  100.7 4.6 %fusion.7 = f32[256,1024]{1,0:T(8,128)S(1)} fusion(bf16[1024,256]{1,0:T(8,128)(2,1)S(1)} %copy-done, f32[1024,1024]{0,1:T(8,128)} %fusion.35, bf16[256,1024]{1,0:T(8,128)(2,1)} %param.11, bf16[256,1024]{1,0:T(8,128)(2,1)S(1)} %copy-done.3), kind=kOutput, calls=%fused_computation.16 | convolution fusion | flops 1083703296 | bytes 6815744 | tf_op jit(solution)/shard_map/dot_general | solution.py:43
  105.3 2.8 %fusion.34 = f32[2,1024,128]{2,1,0:T(8,128)} fusion(f32[2,128,1024]{2,1,0:T(8,128)S(1)} %bitcast.127, f32[2,128,128]{2,1,0:T(8,128)S(1)} %copy-done.4), kind=kOutput, calls=%fused_computation.69 | convolution fusion | flops 402653184 | bytes 2228224 | tf_op jit(solution)/shard_map/fkl,fkc->flc/dot_general | solution.py:47
  108.1 3.1 %copy.26 = f32[2,128,16,64]{3,2,0,1:T(8,128)S(1)} copy(f32[2,128,16,64]{1,3,2,0:T(8,128)} %bitcast.125) | data formatting | bytes 2097152 | tf_op jit(solution)/shard_map/reshape | solution.py:61
  111.2 2.3 %reshape.20 = f32[16,1,16384]{2,1,0:T(1,128)} reshape(f32[128,2,16,64]{3,2,1,0:T(8,128)S(1)} %bitcast.121) | data formatting | bytes 2097152
  113.4 32.0 %all_to_all.38 = f32[16,1,16384]{2,1,0:T(1,128)S(1)} all-to-all(f32[16,1,16384]{2,1,0:T(1,128)} %reshape.20), channel_id=1, replica_groups=mesh['lev'=16,'hor'=32] {'lev'}, dimensions={0} | all-to-all | bytes 2097152 | tf_op jit(solution)/shard_map/all_to_all | solution.py:64
  145.4 4.3 %reduce.1 = f32[16,16384]{1,0:T(8,128)} reduce(f32[16,1,16384]{2,1,0:T(1,128)S(1)} %all_to_all.38, f32[]{:T(128)} %broadcast.42), dimensions={1}, to_apply=%all_to_all.31.reduce_sub_computation | reduce | bytes 2097156 | tf_op jit(solution)/shard_map/all_to_all | solution.py:64
  149.7 2.1 reshape.21
  151.8 2.6 %copy.28 = f32[2,8,16,16,64]{4,3,2,1,0:T(8,128)} copy(f32[2,8,16,16,64]{4,2,0,1,3:T(8,128)S(1)} %bitcast.123) | data formatting | bytes 2097152 | tf_op jit(solution)/shard_map/all_to_all | solution.py:64
  154.3 2.0 all_to_all.34
  156.3 0.1 broadcast_multiply_fusion
  156.4 0.1 fusion.32
  156.5 43.8 %collective-permute-start.3 = (f32[2,8,1,1024]{3,2,1,0:T(1,128)S(1)}, f32[2,8,1,1024]{3,2,1,0:T(1,128)S(1)}, u32[]{:S(2)}, u32[]{:S(2)}) collective-permute-start(f32[2,8,1,1024]{3,2,1,0:T(1,128)S(1)} %get-tuple-element.5), channel_id=1, source_target_pairs={{0,1},{1,2},{2,3},{3,4},{4,5},{5,6},{6,7},{7,8},{8,9},{9,10},{10,1... | collective-permute-start | bytes 196616 | tf_op jit(solution)/shard_map/ppermute | solution.py:12
  200.4 1.9 collective-permute-start.2
  202.3 0.0 collective-permute-done.3
  202.3 6.3 %collective-permute-done.2 = f32[2,8,1,1024]{3,2,1,0:T(1,128)S(1)} collective-permute-done((f32[2,8,1,1024]{3,2,1,0:T(1,128)S(1)}, f32[2,8,1,1024]{3,2,1,0:T(1,128)S(1)}, u32[]{:S(2)}, u32[]{:S(2)}) %collective-permute-start.2) | collective-permute-done | bytes 65568 | tf_op jit(solution)/shard_map/ppermute | solution.py:15
  208.7 0.9 select_maximum_fusion
  209.6 1.7 fusion.9
  (19 shorter events, 0.2 us)
Async XLA Ops:
  0.0 98.0 %copy-start = (bf16[1024,256]{1,0:T(8,128)(2,1)S(1)}, bf16[1024,256]{1,0:T(8,128)(2,1)}, u32[]{:S(2)}) copy-start(bf16[1024,256]{1,0:T(8,128)(2,1)} %param.10) | copy-start | bytes 1572868
  1.4 35.9 %collective-permute-start.1 = (f32[2,8,1,1024]{3,2,1,0:T(1,128)S(1)}, f32[2,8,1,1024]{3,2,1,0:T(1,128)S(1)}, u32[]{:S(2)}, u32[]{:S(2)}) collective-permute-start(f32[2,8,1,1024]{3,2,1,0:T(1,128)S(1)} %get-tuple-element.7), channel_id=1, source_target_pairs={{0,1},{1,2},{2,3},{3,4},{4,5},{5,6},{6,7},{7,8},{8,9},{9,10},{10,1... | collective-permute-start | bytes 196616 | tf_op jit(solution)/shard_map/ppermute | solution.py:12
  4.9 32.4 %collective-permute-start = (f32[2,8,1,1024]{3,2,1,0:T(1,128)S(1)}, f32[2,8,1,1024]{3,2,1,0:T(1,128)S(1)}, u32[]{:S(2)}, u32[]{:S(2)}) collective-permute-start(f32[2,8,1,1024]{3,2,1,0:T(1,128)S(1)} %get-tuple-element.8), channel_id=1, source_target_pairs={{1,0},{2,1},{3,2},{4,3},{5,4},{6,5},{7,6},{8,7},{9,8},{10,9},{11,1... | collective-permute-start | bytes 196616 | tf_op jit(solution)/shard_map/ppermute | solution.py:15
  12.9 24.4 %copy-start.1 = (f32[2,8,16,1024]{3,2,1,0:T(8,128)S(1)}, f32[2,8,16,1024]{3,2,1,0:T(8,128)}, u32[]{:S(2)}) copy-start(f32[2,8,16,1024]{3,2,1,0:T(8,128)} %param.6) | copy-start | bytes 3145732
  19.4 18.8 %copy-start.2 = (f32[8,16,1024]{2,1,0:T(8,128)S(1)}, f32[8,16,1024]{2,1,0:T(8,128)}, u32[]{:S(2)}) copy-start(f32[8,16,1024]{2,1,0:T(8,128)} %param.8) | copy-start | bytes 1572868
  19.4 37.9 %all-to-all-start = ((bf16[16,2,8192]{2,1,0:T(2,128)(2,1)}), bf16[16,2,8192]{2,1,0:T(2,128)(2,1)}, u32[]{:S(2)}, u32[]{:S(2)}) async-start(bf16[16,2,8192]{2,1,0:T(2,128)(2,1)} %reshape.18), calls=%async_computation | async-start | bytes 1048576 | tf_op jit(solution)/shard_map/all_to_all | solution.py:57
  57.4 29.0 %all-to-all-start.1 = ((f32[16,1,16384]{2,1,0:T(1,128)}), f32[16,1,16384]{2,1,0:T(1,128)S(1)}, u32[]{:S(2)}, u32[]{:S(2)}) async-start(f32[16,1,16384]{2,1,0:T(1,128)} %reshape.16), calls=%async_computation.1 | async-start | bytes 2097152 | tf_op jit(solution)/shard_map/all_to_all | solution.py:55
  94.7 2.3 %copy-start.4 = (f32[2,128,128]{2,1,0:T(8,128)S(1)}, f32[2,128,128]{2,1,0:T(8,128)}, u32[]{:S(2)}) copy-start(f32[2,128,128]{2,1,0:T(8,128)} %param.9) | copy-start | bytes 393220
  98.0 2.7 %copy-start.3 = (bf16[256,1024]{1,0:T(8,128)(2,1)S(1)}, bf16[256,1024]{1,0:T(8,128)(2,1)}, u32[]{:S(2)}) copy-start(bf16[256,1024]{1,0:T(8,128)(2,1)} %reshape_reshape.6) | copy-start | bytes 1572868
  156.5 45.8 %collective-permute-start.3 = (f32[2,8,1,1024]{3,2,1,0:T(1,128)S(1)}, f32[2,8,1,1024]{3,2,1,0:T(1,128)S(1)}, u32[]{:S(2)}, u32[]{:S(2)}) collective-permute-start(f32[2,8,1,1024]{3,2,1,0:T(1,128)S(1)} %get-tuple-element.5), channel_id=1, source_target_pairs={{0,1},{1,2},{2,3},{3,4},{4,5},{5,6},{6,7},{7,8},{8,9},{9,10},{10,1... | collective-permute-start | bytes 196616 | tf_op jit(solution)/shard_map/ppermute | solution.py:12
  200.4 8.3 %collective-permute-start.2 = (f32[2,8,1,1024]{3,2,1,0:T(1,128)S(1)}, f32[2,8,1,1024]{3,2,1,0:T(1,128)S(1)}, u32[]{:S(2)}, u32[]{:S(2)}) collective-permute-start(f32[2,8,1,1024]{3,2,1,0:T(1,128)S(1)} %get-tuple-element.6), channel_id=1, source_target_pairs={{1,0},{2,1},{3,2},{4,3},{5,4},{6,5},{7,6},{8,7},{9,8},{10,9},{11,1... | collective-permute-start | bytes 196616 | tf_op jit(solution)/shard_map/ppermute | solution.py:15
